TPU v7x, 256 devices: a whole 4x4x8 slice. The times are simulated.
256 devices in a mesh: seq: 16 (over y, x), chan: 16 (over z, core).
Axes of the slice: x: 4, y: 4, z: 8, core: 2. Of those that a mesh axis runs over, the one named last changes fastest.
Arguments:
- tokens: bfloat16 [57344, 2048], P('seq', 'chan'), may hold values from -6 to 6
- w_query: bfloat16 [2048, 256], replicated, may hold values from -0.125 to 0.125
- w_key: bfloat16 [2048, 256], replicated, may hold values from -0.125 to 0.125
- w_value: bfloat16 [2048, 2048], P(None, 'chan'), may hold values from -0.125 to 0.125
- w_out: bfloat16 [2048, 2048], replicated, may hold values from -0.125 to 0.125
- gain: float32 [2048], replicated, may hold values from 0.1 to 1.9
Outputs:
- mixed: bfloat16 [57344, 2048], P('seq', 'chan')
All inputs are finite; a program needn't handle non-finite values.
Results may differ from a plain program's by a relative error of at most 0.019.
Values may be sent and summed in bfloat16 or wider, within the bound.
A program may use at most 128 MiB of HBM per device.

v0:
```python
import jax
import jax.numpy as jnp
from jax import lax
from jax.sharding import PartitionSpec as P

HEADS = 16
FEAT = 16
HEAD_DIM = 128
BLOCK = 896


def feature_parts(rows):
    linear = rows * FEAT ** (-0.25)
    square = (rows[..., :, None] * rows[..., None, :]).reshape(rows.shape[:-1] + (FEAT * FEAT,)) * (
        2.0 * FEAT
    ) ** (-0.5)
    return (linear, square)


def per_device(tokens, w_query, w_key, w_value, w_out, gain):
    highest = lax.Precision.HIGHEST
    groups = lax.axis_size("chan")
    per_group = HEADS // groups
    my_group = lax.axis_index("chan")
    my_slab = lax.axis_index("seq")
    tok_rows = tokens.shape[0]
    query_cols = per_group * FEAT
    value_cols = per_group * HEAD_DIM
    query_mine = lax.dynamic_slice_in_dim(w_query, my_group * query_cols, query_cols, 1)
    key_mine = lax.dynamic_slice_in_dim(w_key, my_group * query_cols, query_cols, 1)
    initial = (
        jnp.zeros((tok_rows, query_cols), jnp.float32),
        jnp.zeros((tok_rows, query_cols), jnp.float32),
        jnp.zeros((tok_rows, value_cols), jnp.float32),
    )
    piece = lax.all_gather(tokens, "chan", axis=1, tiled=True)
    query_sum, key_sum, value_sum = tuple(
        (
            jnp.dot(piece, weight, preferred_element_type=jnp.float32)
            for weight in (query_mine, key_mine, w_value)
        )
    )
    query_rows = query_sum.astype(jnp.bfloat16)
    key_rows = key_sum.astype(jnp.bfloat16)
    value_rows = value_sum.astype(jnp.bfloat16)
    blocks = tok_rows // BLOCK
    query_blocks = query_rows.reshape(blocks, BLOCK, per_group, FEAT)
    key_blocks = key_rows.reshape(blocks, BLOCK, per_group, FEAT)
    value_blocks = value_rows.reshape(blocks, BLOCK, per_group, HEAD_DIM)
    value_f32 = value_blocks.astype(jnp.float32)
    key_linear, key_square = feature_parts(key_blocks.astype(jnp.float32))
    own_zero = jnp.sum(value_f32, axis=1)
    own_one = jnp.einsum("bthf,bthe->bhfe", key_linear, value_f32, precision=highest)
    own_two = jnp.einsum("bthf,bthe->bhfe", key_square, value_f32, precision=highest)
    own = (own_zero, own_one, own_two)
    slab_total = tuple((jnp.sum(member, axis=0) for member in own))
    initial = tuple((jnp.zeros_like(member) for member in slab_total))
    pieces = (
        lax.all_gather(slab_total[0][None].astype(jnp.bfloat16), "seq", axis=0, tiled=True).astype(
            jnp.float32
        ),
        lax.all_gather(slab_total[1][None].astype(jnp.bfloat16), "seq", axis=0, tiled=True).astype(
            jnp.float32
        ),
        lax.all_gather(slab_total[2][None].astype(jnp.bfloat16), "seq", axis=0, tiled=True).astype(
            jnp.float32
        ),
    )
    count = pieces[0].shape[0]
    order = jnp.arange(count, dtype=jnp.int32)
    earlier_mask = order < my_slab
    prefix = tuple(
        (
            total
            + jnp.sum(
                jnp.where(earlier_mask.reshape((count,) + (1,) * (piece.ndim - 1)), piece, 0.0),
                axis=0,
            )
            for total, piece in zip(initial, pieces)
        )
    )
    earlier = tuple(
        (
            jnp.concatenate([jnp.zeros_like(member[:1]), jnp.cumsum(member, axis=0)[:-1]], axis=0)
            + base[None]
            for member, base in zip(own, prefix)
        )
    )
    query_linear, query_square = feature_parts(query_blocks.astype(jnp.float32))
    inter = earlier[0][:, None] + jnp.einsum(
        "bthf,bhfe->bthe", query_linear, earlier[1], precision=highest
    )
    inter = inter + jnp.einsum("bthf,bhfe->bthe", query_square, earlier[2], precision=highest)
    scores = jnp.einsum(
        "bthf,bshf->bhts", query_blocks, key_blocks, preferred_element_type=jnp.float32
    ) * FEAT ** (-0.5)
    kernel = 1.0 + scores + 0.5 * scores * scores
    causal = jnp.arange(BLOCK)[:, None] >= jnp.arange(BLOCK)[None, :]
    weights = jnp.where(causal, kernel, 0.0).astype(jnp.bfloat16)
    intra = jnp.einsum("bhts,bshe->bthe", weights, value_blocks, preferred_element_type=jnp.float32)
    numerator = (intra + inter).reshape(tok_rows, per_group, HEAD_DIM)
    gain_mine = lax.dynamic_slice_in_dim(gain, my_group * value_cols, value_cols, 0).reshape(
        per_group, HEAD_DIM
    )
    mean_square = jnp.mean(numerator * numerator, axis=-1, keepdims=True)
    hidden = (
        (numerator * lax.rsqrt(mean_square + 1e-05) * gain_mine)
        .astype(jnp.bfloat16)
        .reshape(tok_rows, value_cols)
    )
    out_mine = lax.dynamic_slice_in_dim(w_out, my_group * value_cols, value_cols, 0)
    partial_value = jnp.dot(hidden, out_mine, preferred_element_type=jnp.float32)
    partial_value = lax.optimization_barrier(partial_value.astype(jnp.bfloat16)).astype(jnp.float32)
    mixed = lax.psum_scatter(
        partial_value.astype(jnp.bfloat16), "chan", scatter_dimension=1, tiled=True
    )
    return mixed


def solution(mesh):
    return jax.shard_map(
        per_device,
        mesh=mesh,
        in_specs=(P("seq", "chan"), P(), P(), P(None, "chan"), P(), P()),
        out_specs=P("seq", "chan"),
        check_vma=False,
    )
```

profile of v0, /device:TPU:2, one launch (start us, length us, event | category | flops | bytes accessed | tf_op | source)
XLA Modules:
  0.0 357.5 jit_solution(1797674125439511556)
XLA Ops:
  6.5 0.0 copy-start
  6.5 0.0 all-gather.7.cloned.1.call-start
  6.5 0.7 all-gather.7.cloned.1.call-update
  7.3 0.0 all-gather.9.cloned.1.call-start
  7.3 0.8 dynamic_slice.14
  8.1 0.2 iota_compare_fusion
  8.3 96.7 %all-gather.7.cloned.1.call-done = bf16[3584,2048]{1,0:T(8,128)(2,1)} async-done(((bf16[3584,128]{1,0:T(8,128)(2,1)}), bf16[3584,2048]{1,0:T(8,128)(2,1)}) %all-gather.7.cloned.1.call-update) | async-done | bytes 14680080 | tf_op jit(solution)/shard_map/all_gather | solution.py:36
  105.0 9.2 %fusion.51 = (bf16[128]{0:T(256)(128)(2,1)S(1)}, bf16[3584,128]{1,0:T(8,128)(2,1)S(1)}) fusion(bf16[3584,2048]{1,0:T(8,128)(2,1)} %all-gather.7.cloned.1.call-done, bf16[2048,128]{1,0:T(8,128)(2,1)} %param.9), kind=kOutput, calls=%fused_computation.68 | convolution fusion | flops 1879965568 | bytes 16122112 | tf_op jit(solution)/shard_map/dot_general | solution.py:39
  114.3 0.1 convert_reduce_fusion
  114.4 0.0 copy-done
  114.4 9.4 %convolution_convert_fusion.2 = bf16[16,3584]{1,0:T(8,128)(2,1)S(1)} fusion(bf16[3584,2048]{1,0:T(8,128)(2,1)} %all-gather.7.cloned.1.call-done, bf16[2048,256]{1,0:T(8,128)(2,1)S(1)} %copy-done, s32[]{:T(128)S(6)} %select_n.25), kind=kOutput, calls=%fused_computation.3 | convolution fusion | flops 234938368 | bytes 15319044 | tf_op jit(solution)/shard_map/dot_general | solution.py:39
  123.8 0.5 fusion.50
  124.4 20.3 %all-gather.3 = bf16[16,1,128]{2,1,0:T(2,128)(2,1)S(1)} all-gather(bf16[1,1,128]{2,1,0:T(2,128)(2,1)S(1)} %bitcast.100), channel_id=2, replica_groups=mesh['seq'=16,'chan'=16] {'seq'}, dimensions={0}, use_global_device_ids=true | all-gather | bytes 4352 | tf_op jit(solution)/shard_map/all_gather | solution.py:59
  144.7 0.1 fusion.32
  144.8 0.0 copy-start.3
  144.8 21.4 %all-gather.1 = bf16[256,128]{1,0:T(8,128)(2,1)S(1)} all-gather(bf16[16,128]{1,0:T(8,128)(2,1)S(1)} %get-tuple-element.7), channel_id=3, replica_groups=mesh['seq'=16,'chan'=16] {'seq'}, dimensions={0}, use_global_device_ids=true | all-gather | bytes 69632 | tf_op jit(solution)/shard_map/all_gather | solution.py:62
  166.2 0.4 multiply_multiply_fusion.1
  166.6 2.5 fusion.49
  169.0 0.0 copy-done.3
  169.0 0.0 all-gather.9.cloned.1.call-update
  169.1 0.0 reduce-scatter.4.cloned.1.call-start
  169.1 0.4 fusion.8
  169.5 0.0 copy-start.2
  169.6 0.1 fusion.20
  169.7 0.1 fusion.37
  169.8 0.0 slice-start.1
  169.8 9.6 %convolution_convert_fusion.3 = bf16[16,3584]{1,0:T(8,128)(2,1)S(1)} fusion(bf16[3584,2048]{1,0:T(8,128)(2,1)} %all-gather.7.cloned.1.call-done, bf16[2048,256]{1,0:T(8,128)(2,1)} %param.7, s32[]{:T(128)S(6)} %select_n.25), kind=kOutput, calls=%fused_computation.4 | convolution fusion | flops 234938368 | bytes 15319044 | tf_op jit(solution)/shard_map/dot_general | solution.py:39
  179.4 0.0 copy-done.2
  179.4 0.0 slice-done.1
  179.4 0.0 slice-start
  179.4 2.9 fusion.16
  182.3 2.2 multiply_multiply_fusion
  184.5 29.4 %all-gather.9.cloned.1.call-done = bf16[4096,128]{1,0:T(8,128)(2,1)} async-done(((bf16[256,128]{1,0:T(8,128)(2,1)}), bf16[4096,128]{1,0:T(8,128)(2,1)}) %all-gather.9.cloned.1.call-update) | async-done | bytes 1048592 | tf_op jit(solution)/shard_map/all_gather | solution.py:65
  213.9 1.5 fusion
  215.4 0.0 slice-done
  215.4 5.6 %fusion.6 = f32[4,128,896]{2,1,0:T(8,128)} fusion(f32[4,896,256]{1,2,0:T(8,128)} %bitcast.84, f32[3,1,256,128]{3,2,0,1:T(8,128)S(1)} %slice-done, f32[256,128]{1,0:T(8,128)S(1)} %fusion), kind=kOutput, calls=%fused_computation.20 | convolution fusion | flops 1409417216 | bytes 6029312 | tf_op jit(solution)/shard_map/bthf,bhfe->bthe/dot_general | solution.py:93
  221.0 8.5 %multiply_reduce_fusion = (f32[4,896]{1,0:T(4,128)S(1)}, f32[4,896,1,128]{1,3,0,2:T(8,128)}) fusion(f32[4,128,896]{2,1,0:T(8,128)} %fusion.6, f32[4,128,896]{2,1,0:T(8,128)} %fusion.16, f32[4,128]{1,0:T(4,128)S(1)} %add_bitcast_fusion, bf16[4,896,128]{2,1,0:T(8,128)(2,1)S(1)} %bitcast.88, pred[896,896]{1,0:T(8,128)(4,1)S(1)} %iota_compare_fusion, ...), kind=kOutput, calls=%fused_computation.18 | convolution fusion | flops 949613056 | bytes 7471104 | tf_op jit(solution)/shard_map/bhts,bshe->bthe/dot_general | solution.py:100
  229.5 1.8 copy.41
  231.3 0.5 fusion.3
  231.9 8.3 %convolution_convert_fusion = bf16[3584,2048]{1,0:T(8,128)(2,1)} fusion(bf16[3584,128]{1,0:T(8,128)(2,1)S(1)} %fusion.3, bf16[2048,2048]{1,0:T(8,128)(2,1)} %param.10, s32[]{:T(128)S(6)} %select_n.30), kind=kOutput, calls=%fused_computation | convolution fusion | flops 1886388224 | bytes 16121860 | tf_op jit(solution)/shard_map/dot_general | solution.py:112
  240.2 18.8 %copy.45 = bf16[3584,2048]{0,1:T(8,128)(2,1)} copy(bf16[3584,2048]{1,0:T(8,128)(2,1)} %convolution_convert_fusion) | data formatting | bytes 29360128
  259.0 0.0 reduce-scatter.4.cloned.1.call-update
  259.0 0.0 copy-start.1
  259.0 89.8 %reduce-scatter.4.cloned.1.call-done = bf16[128,3584]{1,0:T(8,128)(2,1)} async-done(((bf16[2048,3584]{1,0:T(8,128)(2,1)}), bf16[128,3584]{1,0:T(8,128)(2,1)}) %reduce-scatter.4.cloned.1.call-update) | async-done | bytes 917520
  348.8 2.2 copy.46
  351.0 0.0 copy-done.1
  (7 shorter events, 0.1 us)
Async XLA Ops:
  6.5 107.9 %copy-start = (bf16[2048,256]{1,0:T(8,128)(2,1)S(1)}, bf16[2048,256]{1,0:T(8,128)(2,1)}, u32[]{:S(2)}) copy-start(bf16[2048,256]{1,0:T(8,128)(2,1)} %param.8) | copy-start | bytes 3145732
  6.5 98.5 %all-gather.7.cloned.1.call-start = ((), (), s32[]{:S(2)}) async-start(), calls=%async_computation.1 | async-start | bytes 15597568 | tf_op jit(solution)/shard_map/all_gather | solution.py:36
  7.3 206.7 %all-gather.9.cloned.1.call-start = ((), (), s32[]{:S(2)}) async-start(), calls=%async_computation.2 | async-start | bytes 1114112 | tf_op jit(solution)/shard_map/all_gather | solution.py:65
  144.8 24.3 %copy-start.3 = (f32[4,1,16,128]{3,2,0,1:T(8,128)}, f32[4,1,16,128]{3,2,0,1:T(8,128)S(1)}, u32[]{:S(2)}) copy-start(f32[4,1,16,128]{3,2,0,1:T(8,128)S(1)} %fusion.32) | copy-start | bytes 98308
  169.1 179.7 %reduce-scatter.4.cloned.1.call-start = ((), (), s32[]{:S(2)}) async-start(), calls=%async_computation.3 | async-start | bytes 15597568
  169.5 9.9 %copy-start.2 = (f32[4,1,256,128]{3,2,0,1:T(8,128)}, f32[4,1,256,128]{3,2,0,1:T(8,128)S(1)}, u32[]{:S(2)}) copy-start(f32[4,1,256,128]{3,2,0,1:T(8,128)S(1)} %fusion.8) | copy-start | bytes 1572868
  169.8 9.6 %slice-start.1 = ((f32[4,1,16,128]{3,2,0,1:T(8,128)}), f32[3,1,16,128]{3,2,0,1:T(8,128)S(1)}, s32[]{:S(2)}) async-start(f32[4,1,16,128]{3,2,0,1:T(8,128)} %copy-done.3), calls=%async_computation.5 | async-start | bytes 49152 | tf_op jit(solution)/shard_map/slice | solution.py:84
  179.4 36.0 %slice-start = ((f32[4,1,256,128]{3,2,0,1:T(8,128)}), f32[3,1,256,128]{3,2,0,1:T(8,128)S(1)}, s32[]{:S(2)}) async-start(f32[4,1,256,128]{3,2,0,1:T(8,128)} %copy-done.2), calls=%async_computation.4 | async-start | bytes 786432 | tf_op jit(solution)/shard_map/slice | solution.py:84
  259.0 92.0 %copy-start.1 = (bf16[2048,256]{1,0:T(8,128)(2,1)S(1)}, bf16[2048,256]{1,0:T(8,128)(2,1)}, u32[]{:S(2)}) copy-start(bf16[2048,256]{1,0:T(8,128)(2,1)} %param.8) | copy-start | bytes 3145732
Sparse Core Ops, SparseCore 0:
  9.1 95.8 all-gather.6
  169.2 44.6 all-gather.8
  259.1 89.6 reduce-scatter.3
where the time goes:
time: 358 us
  waiting for transfers between devices  217 us (61%)
  matrix products  56.4 us (16%)
  blocking collectives  41.7 us (12%)
  local copies, waits for them, and re-layouts  23.6 us (7%)
  between operations  13.3 us (4%)
  other arithmetic  5.75 us (2%)
    all_gather x1, waiting for transfers between devices, per_device(): piece = lax.all_gather(tokens, 'chan', axis=1, tiled=True)  96.7 us
    unnamed x4, waiting for transfers between devices  90.5 us
    all_gather x1, waiting for transfers between devices, per_device(): lax.all_gather(slab_total[2][None].astype(jnp.bfloat16), 'seq', axis=0, t...  29.4 us
    dot_general x3, matrix products, per_device(): jnp.dot(piece, weight, preferred_element_type=jnp.float32)  28.2 us
    all_gather x1, blocking collectives, per_device(): lax.all_gather(slab_total[1][None].astype(jnp.bfloat16), 'seq', axis=0, t...  21.4 us
    unnamed x10, local copies, waits for them, and re-layouts  21 us
    all_gather x1, blocking collectives, per_device(): lax.all_gather(slab_total[0][None].astype(jnp.bfloat16), 'seq', axis=0, t...  20.3 us
    dot_general x1, matrix products, per_device(): jnp.einsum('bhts,bshe->bthe', weights, value_blocks, preferred_element_ty...  8.45 us
  transfers between devices with their start and end apart: 3, of which 3 were waited for; matrix products, arithmetic and copies ran while one was open for 5% of the time, Pallas kernels for 0%

commit v1 on v0

--- a/solution.py
+++ b/solution.py
@@ -7,6 +7,19 @@
 FEAT = 16
 HEAD_DIM = 128
 BLOCK = 896
+
+
+def gather_around(x, axis, dim):
+    ways = lax.axis_size(axis)
+    up = [(d, (d + 1) % ways) for d in range(ways)]
+    down = [(d, (d - 1) % ways) for d in range(ways)]
+    earlier, later = ([x], [x])
+    for _ in range(ways // 2):
+        earlier.append(lax.ppermute(earlier[-1], axis, up))
+    for _ in range((ways - 1) // 2):
+        later.append(lax.ppermute(later[-1], axis, down))
+    line = jnp.concatenate([*earlier[::-1], *later[1:]], axis=dim)
+    return jnp.roll(line, (lax.axis_index(axis) - ways // 2) * x.shape[dim], axis=dim)
 
 
 def feature_parts(rows):
@@ -33,7 +46,7 @@
         jnp.zeros((tok_rows, query_cols), jnp.float32),
         jnp.zeros((tok_rows, value_cols), jnp.float32),
     )
-    piece = lax.all_gather(tokens, "chan", axis=1, tiled=True)
+    piece = gather_around(tokens, "chan", 1)
     query_sum, key_sum, value_sum = tuple(
         (
             jnp.dot(piece, weight, preferred_element_type=jnp.float32)

time: 358 us -> 402 us (1.12)
  local copies, waits for them, and re-layouts: 23.6 us -> 83.1 us
  waiting for transfers between devices: 217 us -> 179 us
  starting transfers between devices: 0.08 us -> 21.6 us
    all_gather x1 -> x0, waiting for transfers between devices: 96.7 us -> none  [per_device(): piece = lax.all_gather(tokens, 'chan', axis=1, tiled=True)]
    ppermute x0 -> x15, waiting for transfers between devices: none -> 89.9 us  [the longest x8 85.5 us: gather_around(): earlier.append(lax.ppermute(earlier[-1], axis, up))]
    unnamed x10 -> x69, local copies, waits for them, and re-layouts: 21 us -> 79.2 us
    all_gather x1, waiting for transfers between devices: 29.4 us -> 0.01 us  [per_device(): lax.all_gather(slab_total[2][None].astype(jnp.bfloat16), 'seq', axis=0, t...]
    ppermute x0 -> x15, starting transfers between devices: none -> 21.5 us  [the longest x7 21.5 us: gather_around(): later.append(lax.ppermute(later[-1], axis, down))]
    unnamed x4 -> x3, waiting for transfers between devices: 90.5 us -> 89 us
  transfers between devices with their start and end apart: 3 -> 17, of which waited for: 3 -> 14; matrix products, arithmetic and copies ran while one was open for 5% -> 12% of each run, Pallas kernels for 0% -> 0%
where the time goes in v1:
time: 402 us; the launch traced here: 400 us
  waiting for transfers between devices  179 us (45%)
  local copies, waits for them, and re-layouts  83.1 us (21%)
  matrix products  54.2 us (13%)
  blocking collectives  42.2 us (10%)
  starting transfers between devices  21.6 us (5%)
  between operations  13.6 us (3%)
  other arithmetic  6.48 us (2%)
    unnamed x3, waiting for transfers between devices  89 us
    ppermute x8, waiting for transfers between devices, gather_around(): earlier.append(lax.ppermute(earlier[-1], axis, up))  85.5 us
    unnamed x69, local copies, waits for them, and re-layouts  79.2 us
    dot_general x3, matrix products, per_device(): jnp.dot(piece, weight, preferred_element_type=jnp.float32)  26.2 us
    all_gather x1, blocking collectives, per_device(): lax.all_gather(slab_total[1][None].astype(jnp.bfloat16), 'seq', axis=0, t...  21.6 us
    ppermute x7, starting transfers between devices, gather_around(): later.append(lax.ppermute(later[-1], axis, down))  21.5 us
    all_gather x1, blocking collectives, per_device(): lax.all_gather(slab_total[0][None].astype(jnp.bfloat16), 'seq', axis=0, t...  20.6 us
    dot_general x1, matrix products, per_device(): jnp.dot(hidden, out_mine, preferred_element_type=jnp.float32)  8.29 us
  transfers between devices with their start and end apart: 17, of which 14 were waited for; matrix products, arithmetic and copies ran while one was open for 12% of the time, Pallas kernels for 0%

profile of v1, /device:TPU:2, one launch (start us, length us, event | category | flops | bytes accessed | tf_op | source)
XLA Modules:
  0.0 400.0 jit_solution(15196121008816614359)
XLA Ops:
  6.6 16.6 %collective-permute-done = bf16[3584,128]{1,0:T(8,128)(2,1)S(1)} collective-permute-done((bf16[3584,128]{1,0:T(8,128)(2,1)}, bf16[3584,128]{1,0:T(8,128)(2,1)S(1)}, u32[]{:S(2)}, u32[]{:S(2)}) %collective-permute-start) | collective-permute-done | bytes 917536 | tf_op jit(solution)/shard_map/ppermute | solution.py:18
  23.2 3.0 collective-permute-start.8
  26.1 11.2 %collective-permute-done.1 = bf16[3584,128]{1,0:T(8,128)(2,1)} collective-permute-done((bf16[3584,128]{1,0:T(8,128)(2,1)S(1)}, bf16[3584,128]{1,0:T(8,128)(2,1)}, u32[]{:S(2)}, u32[]{:S(2)}) %collective-permute-start.1) | collective-permute-done | bytes 917536 | tf_op jit(solution)/shard_map/ppermute | solution.py:18
  37.3 3.1 collective-permute-start.9
  40.5 11.1 %collective-permute-done.2 = bf16[3584,128]{1,0:T(8,128)(2,1)S(1)} collective-permute-done((bf16[3584,128]{1,0:T(8,128)(2,1)}, bf16[3584,128]{1,0:T(8,128)(2,1)S(1)}, u32[]{:S(2)}, u32[]{:S(2)}) %collective-permute-start.2) | collective-permute-done | bytes 917536 | tf_op jit(solution)/shard_map/ppermute | solution.py:18
  51.7 1.1 copy-done.2
  52.8 2.9 collective-permute-start.10
  55.7 9.9 %collective-permute-done.3 = bf16[3584,128]{1,0:T(8,128)(2,1)S(1)} collective-permute-done((bf16[3584,128]{1,0:T(8,128)(2,1)S(1)}, bf16[3584,128]{1,0:T(8,128)(2,1)S(1)}, u32[]{:S(2)}, u32[]{:S(2)}) %collective-permute-start.3) | collective-permute-done | bytes 917536 | tf_op jit(solution)/shard_map/ppermute | solution.py:18
  66.6 3.1 collective-permute-start.11
  69.7 9.9 %collective-permute-done.4 = bf16[3584,128]{1,0:T(8,128)(2,1)S(1)} collective-permute-done((bf16[3584,128]{1,0:T(8,128)(2,1)S(1)}, bf16[3584,128]{1,0:T(8,128)(2,1)S(1)}, u32[]{:S(2)}, u32[]{:S(2)}) %collective-permute-start.4) | collective-permute-done | bytes 917536 | tf_op jit(solution)/shard_map/ppermute | solution.py:18
  81.5 3.1 collective-permute-start.12
  84.7 9.0 %collective-permute-done.5 = bf16[3584,128]{1,0:T(8,128)(2,1)S(1)} collective-permute-done((bf16[3584,128]{1,0:T(8,128)(2,1)S(1)}, bf16[3584,128]{1,0:T(8,128)(2,1)S(1)}, u32[]{:S(2)}, u32[]{:S(2)}) %collective-permute-start.5) | collective-permute-done | bytes 917536 | tf_op jit(solution)/shard_map/ppermute | solution.py:18
  93.6 1.9 collective-permute-done.12
  95.6 3.2 collective-permute-start.13
  98.8 9.0 %collective-permute-done.6 = bf16[3584,128]{1,0:T(8,128)(2,1)} collective-permute-done((bf16[3584,128]{1,0:T(8,128)(2,1)S(1)}, bf16[3584,128]{1,0:T(8,128)(2,1)}, u32[]{:S(2)}, u32[]{:S(2)}) %collective-permute-start.6) | collective-permute-done | bytes 917536 | tf_op jit(solution)/shard_map/ppermute | solution.py:18
  108.8 1.1 iota_compare_fusion
  110.0 3.1 collective-permute-start.14
  113.1 9.0 %collective-permute-done.7 = bf16[3584,128]{1,0:T(8,128)(2,1)} collective-permute-done((bf16[3584,128]{1,0:T(8,128)(2,1)}, bf16[3584,128]{1,0:T(8,128)(2,1)}, u32[]{:S(2)}, u32[]{:S(2)}) %collective-permute-start.7) | collective-permute-done | bytes 917536 | tf_op jit(solution)/shard_map/ppermute | solution.py:18
  122.1 2.2 constant_dynamic-update-slice_fusion.31
  124.4 2.2 constant_dynamic-update-slice_fusion.30
  126.6 2.2 constant_dynamic-update-slice_fusion.29
  128.8 2.2 constant_dynamic-update-slice_fusion.28
  131.0 2.2 constant_dynamic-update-slice_fusion.27
  133.2 2.2 constant_dynamic-update-slice_fusion.26
  135.5 2.3 constant_dynamic-update-slice_fusion.25
  137.7 1.0 constant_dynamic-update-slice_fusion.24
  138.7 2.2 constant_dynamic-update-slice_fusion.23
  140.9 2.2 constant_dynamic-update-slice_fusion.22
  143.1 2.2 constant_dynamic-update-slice_fusion.21
  145.3 2.2 constant_dynamic-update-slice_fusion.20
  147.5 2.3 constant_dynamic-update-slice_fusion.19
  149.8 2.2 constant_dynamic-update-slice_fusion.18
  152.0 2.2 constant_dynamic-update-slice_fusion.17
  154.2 1.1 constant_dynamic-update-slice_fusion.16
  155.3 2.2 constant_dynamic-update-slice_fusion.15
  157.5 2.2 constant_dynamic-update-slice_fusion.14
  159.7 1.1 constant_dynamic-update-slice_fusion.13
  160.8 1.0 constant_dynamic-update-slice_fusion.12
  161.9 1.1 constant_dynamic-update-slice_fusion.11
  162.9 1.1 constant_dynamic-update-slice_fusion.10
  164.0 2.2 constant_dynamic-update-slice_fusion.9
  167.3 1.1 constant_dynamic-update-slice_fusion.7
  168.4 2.2 constant_dynamic-update-slice_fusion.6
  170.6 1.1 constant_dynamic-update-slice_fusion.5
  171.7 1.1 constant_dynamic-update-slice_fusion.4
  173.8 2.2 constant_dynamic-update-slice_fusion.2
  176.1 2.3 constant_dynamic-update-slice_fusion.1
  178.3 1.1 constant_dynamic-update-slice_fusion
  179.4 7.8 %fusion.67 = (bf16[128]{0:T(256)(128)(2,1)S(1)}, bf16[3584,128]{1,0:T(8,128)(2,1)S(1)}) fusion(bf16[2048,128]{1,0:T(8,128)(2,1)S(1)} %copy-done.17, bf16[3584,4096]{1,0:T(8,128)(2,1)} %constant_dynamic-update-slice_fusion, s32[]{:T(128)S(6)} %select_n.39), kind=kOutput, calls=%fused_computation.107 | convolution fusion | flops 1879965568 | bytes 16122116 | tf_op jit(solution)/shard_map/dot_general | solution.py:52
  187.2 9.2 %fusion.12 = bf16[3584,16]{0,1:T(8,128)(2,1)S(1)} fusion(bf16[3584,4096]{1,0:T(8,128)(2,1)} %constant_dynamic-update-slice_fusion, s32[]{:T(128)S(6)} %select_n.39, bf16[2048,256]{1,0:T(8,128)(2,1)S(1)} %copy-done, s32[]{:T(128)S(6)} %select_n.40), kind=kOutput, calls=%fused_computation.10 | convolution fusion | flops 234938368 | bytes 15319048 | tf_op jit(solution)/shard_map/dot_general | solution.py:52
  197.5 2.5 fusion.65
  200.5 20.6 %all-gather.3 = bf16[16,1,128]{2,1,0:T(2,128)(2,1)S(1)} all-gather(bf16[1,1,128]{2,1,0:T(2,128)(2,1)S(1)} %bitcast.95), channel_id=2, replica_groups=mesh['seq'=16,'chan'=16] {'seq'}, dimensions={0}, use_global_device_ids=true | all-gather | bytes 4352 | tf_op jit(solution)/shard_map/all_gather | solution.py:72
  221.1 21.6 %all-gather.1 = bf16[256,128]{1,0:T(8,128)(2,1)S(1)} all-gather(bf16[16,128]{1,0:T(8,128)(2,1)S(1)} %get-tuple-element.7), channel_id=3, replica_groups=mesh['seq'=16,'chan'=16] {'seq'}, dimensions={0}, use_global_device_ids=true | all-gather | bytes 69632 | tf_op jit(solution)/shard_map/all_gather | solution.py:75
  242.9 9.3 %fusion.9 = bf16[3584,16]{0,1:T(8,128)(2,1)S(1)} fusion(bf16[3584,4096]{1,0:T(8,128)(2,1)} %constant_dynamic-update-slice_fusion, s32[]{:T(128)S(6)} %select_n.39, bf16[2048,256]{1,0:T(8,128)(2,1)} %param.7, s32[]{:T(128)S(6)} %select_n.40), kind=kOutput, calls=%fused_computation.9 | convolution fusion | flops 234938368 | bytes 15319048 | tf_op jit(solution)/shard_map/dot_general | solution.py:52
  252.2 2.9 fusion.31
  255.1 2.2 multiply_multiply_fusion
  257.3 1.5 fusion.15
  258.8 5.6 %fusion.21 = f32[4,128,896]{2,1,0:T(8,128)} fusion(f32[4,896,256]{1,2,0:T(8,128)} %bitcast.79, f32[3,1,256,128]{3,2,0,1:T(8,128)S(1)} %slice.13, f32[256,128]{1,0:T(8,128)S(1)} %fusion.15), kind=kOutput, calls=%fused_computation.26 | convolution fusion | flops 1409417216 | bytes 6029312 | tf_op jit(solution)/shard_map/bthf,bhfe->bthe/dot_general | solution.py:106
  264.4 8.2 %multiply_reduce_fusion = (f32[4,896]{1,0:T(4,128)S(1)}, f32[4,896,1,128]{1,3,0,2:T(8,128)}) fusion(f32[4,128,896]{2,1,0:T(8,128)} %fusion.21, f32[4,128,896]{2,1,0:T(8,128)} %fusion.31, f32[4,128]{1,0:T(4,128)S(1)} %add_bitcast_fusion, bf16[4,896,128]{2,1,0:T(8,128)(2,1)S(1)} %bitcast.83, pred[896,896]{1,0:T(8,128)(4,1)S(1)} %copy-done.16, ...), kind=kOutput, calls=%fused_computation.24 | convolution fusion | flops 949613056 | bytes 7471104 | tf_op jit(solution)/shard_map/bhts,bshe->bthe/dot_general | solution.py:113
  272.5 1.8 copy.41
  274.9 8.3 %convolution_convert_fusion = bf16[3584,2048]{1,0:T(8,128)(2,1)} fusion(bf16[3584,128]{1,0:T(8,128)(2,1)S(1)} %fusion.18, bf16[2048,2048]{1,0:T(8,128)(2,1)} %param.10, s32[]{:T(128)S(6)} %select_n.45), kind=kOutput, calls=%fused_computation | convolution fusion | flops 1886388224 | bytes 16121860 | tf_op jit(solution)/shard_map/dot_general | solution.py:125
  283.2 18.7 %copy.45 = bf16[3584,2048]{0,1:T(8,128)(2,1)} copy(bf16[3584,2048]{1,0:T(8,128)(2,1)} %convolution_convert_fusion) | data formatting | bytes 29360128
  302.0 89.0 %reduce-scatter.4.cloned.1.call-done = bf16[128,3584]{1,0:T(8,128)(2,1)} async-done(((bf16[2048,3584]{1,0:T(8,128)(2,1)}), bf16[128,3584]{1,0:T(8,128)(2,1)}) %reduce-scatter.4.cloned.1.call-update) | async-done | bytes 917520
  391.0 2.2 copy.46
  (74 shorter events, 8.7 us)
Async XLA Ops:
  6.5 180.7 %copy-start = (bf16[2048,256]{1,0:T(8,128)(2,1)S(1)}, bf16[2048,256]{1,0:T(8,128)(2,1)}, u32[]{:S(2)}) copy-start(bf16[2048,256]{1,0:T(8,128)(2,1)} %param.8) | copy-start | bytes 3145732
  6.5 160.7 %copy-start.1 = (bf16[3584,128]{1,0:T(8,128)(2,1)S(1)}, bf16[3584,128]{1,0:T(8,128)(2,1)}, u32[]{:S(2)}) copy-start(bf16[3584,128]{1,0:T(8,128)(2,1)} %param.6) | copy-start | bytes 2752516
  6.5 250.7 %all-gather.6.cloned.1.call-start = ((), (), s32[]{:S(2)}) async-start(), calls=%async_computation.1 | async-start | bytes 1114112 | tf_op jit(solution)/shard_map/all_gather | solution.py:78
  6.5 16.6 %collective-permute-start = (bf16[3584,128]{1,0:T(8,128)(2,1)}, bf16[3584,128]{1,0:T(8,128)(2,1)S(1)}, u32[]{:S(2)}, u32[]{:S(2)}) collective-permute-start(bf16[3584,128]{1,0:T(8,128)(2,1)} %param.6), channel_id=1, source_target_pairs={{0,1},{1,2},{2,3},{3,4},{4,5},{5,6},{6,7},{7,8},{8,9},{9,10},{10,1... | collective-permute-start | bytes 2752520 | tf_op jit(solution)/shard_map/ppermute | solution.py:18
  23.2 14.1 %collective-permute-start.1 = (bf16[3584,128]{1,0:T(8,128)(2,1)S(1)}, bf16[3584,128]{1,0:T(8,128)(2,1)}, u32[]{:S(2)}, u32[]{:S(2)}) collective-permute-start(bf16[3584,128]{1,0:T(8,128)(2,1)S(1)} %collective-permute-done), channel_id=1, source_target_pairs={{0,1},{1,2},{2,3},{3,4},{4,5},{5,6},{6,7},{7,8},{8,9},{9,10},{10,1... | collective-permute-start | bytes 2752520 | tf_op jit(solution)/shard_map/ppermute | solution.py:18
  23.2 14.2 %collective-permute-start.8 = (bf16[3584,128]{1,0:T(8,128)(2,1)}, bf16[3584,128]{1,0:T(8,128)(2,1)}, u32[]{:S(2)}, u32[]{:S(2)}) collective-permute-start(bf16[3584,128]{1,0:T(8,128)(2,1)} %param.6), channel_id=1, source_target_pairs={{0,15},{1,0},{2,1},{3,2},{4,3},{5,4},{6,5},{7,6},{8,7},{9,8},{10,9... | collective-permute-start | bytes 2752520 | tf_op jit(solution)/shard_map/ppermute | solution.py:20
  37.3 14.2 %collective-permute-start.2 = (bf16[3584,128]{1,0:T(8,128)(2,1)}, bf16[3584,128]{1,0:T(8,128)(2,1)S(1)}, u32[]{:S(2)}, u32[]{:S(2)}) collective-permute-start(bf16[3584,128]{1,0:T(8,128)(2,1)} %collective-permute-done.1), channel_id=1, source_target_pairs={{0,1},{1,2},{2,3},{3,4},{4,5},{5,6},{6,7},{7,8},{8,9},{9,10},{10,1... | collective-permute-start | bytes 2752520 | tf_op jit(solution)/shard_map/ppermute | solution.py:18
  37.3 14.3 %collective-permute-start.9 = (bf16[3584,128]{1,0:T(8,128)(2,1)}, bf16[3584,128]{1,0:T(8,128)(2,1)S(1)}, u32[]{:S(2)}, u32[]{:S(2)}) collective-permute-start(bf16[3584,128]{1,0:T(8,128)(2,1)} %collective-permute-done.8), channel_id=1, source_target_pairs={{0,15},{1,0},{2,1},{3,2},{4,3},{5,4},{6,5},{7,6},{8,7},{9,8},{10,9... | collective-permute-start | bytes 2752520 | tf_op jit(solution)/shard_map/ppermute | solution.py:20
  51.5 15.1 %copy-start.4 = (bf16[3584,128]{1,0:T(8,128)(2,1)}, bf16[3584,128]{1,0:T(8,128)(2,1)S(1)}, u32[]{:S(2)}) copy-start(bf16[3584,128]{1,0:T(8,128)(2,1)S(1)} %collective-permute-done.2) | copy-start | bytes 2752516
  51.5 14.0 %collective-permute-start.3 = (bf16[3584,128]{1,0:T(8,128)(2,1)S(1)}, bf16[3584,128]{1,0:T(8,128)(2,1)S(1)}, u32[]{:S(2)}, u32[]{:S(2)}) collective-permute-start(bf16[3584,128]{1,0:T(8,128)(2,1)S(1)} %collective-permute-done.2), channel_id=1, source_target_pairs={{0,1},{1,2},{2,3},{3,4},{4,5},{5,6},{6,7},{7,8},{8,9},{9,10},{10,1... | collective-permute-start | bytes 2752520 | tf_op jit(solution)/shard_map/ppermute | solution.py:18
  51.7 1.1 copy-start.2
  52.8 13.8 %collective-permute-start.10 = (bf16[3584,128]{1,0:T(8,128)(2,1)S(1)}, bf16[3584,128]{1,0:T(8,128)(2,1)S(1)}, u32[]{:S(2)}, u32[]{:S(2)}) collective-permute-start(bf16[3584,128]{1,0:T(8,128)(2,1)S(1)} %collective-permute-done.9), channel_id=1, source_target_pairs={{0,15},{1,0},{2,1},{3,2},{4,3},{5,4},{6,5},{7,6},{8,7},{9,8},{10,9... | collective-permute-start | bytes 2752520 | tf_op jit(solution)/shard_map/ppermute | solution.py:20
  65.6 30.0 %copy-start.10 = (bf16[3584,128]{1,0:T(8,128)(2,1)}, bf16[3584,128]{1,0:T(8,128)(2,1)S(1)}, u32[]{:S(2)}) copy-start(bf16[3584,128]{1,0:T(8,128)(2,1)S(1)} %collective-permute-done.3) | copy-start | bytes 2752516
  65.6 14.0 %collective-permute-start.4 = (bf16[3584,128]{1,0:T(8,128)(2,1)S(1)}, bf16[3584,128]{1,0:T(8,128)(2,1)S(1)}, u32[]{:S(2)}, u32[]{:S(2)}) collective-permute-start(bf16[3584,128]{1,0:T(8,128)(2,1)S(1)} %collective-permute-done.3), channel_id=1, source_target_pairs={{0,1},{1,2},{2,3},{3,4},{4,5},{5,6},{6,7},{7,8},{8,9},{9,10},{10,1... | collective-permute-start | bytes 2752520 | tf_op jit(solution)/shard_map/ppermute | solution.py:18
  66.6 3.1 copy-start.6
  66.6 14.0 %collective-permute-start.11 = (bf16[3584,128]{1,0:T(8,128)(2,1)S(1)}, bf16[3584,128]{1,0:T(8,128)(2,1)S(1)}, u32[]{:S(2)}, u32[]{:S(2)}) collective-permute-start(bf16[3584,128]{1,0:T(8,128)(2,1)S(1)} %collective-permute-done.10), channel_id=1, source_target_pairs={{0,15},{1,0},{2,1},{3,2},{4,3},{5,4},{6,5},{7,6},{8,7},{9,8},{10,9... | collective-permute-start | bytes 2752520 | tf_op jit(solution)/shard_map/ppermute | solution.py:20
  79.6 19.2 %copy-start.12 = (bf16[3584,128]{1,0:T(8,128)(2,1)}, bf16[3584,128]{1,0:T(8,128)(2,1)S(1)}, u32[]{:S(2)}) copy-start(bf16[3584,128]{1,0:T(8,128)(2,1)S(1)} %collective-permute-done.4) | copy-start | bytes 2752516
  79.6 14.0 %collective-permute-start.5 = (bf16[3584,128]{1,0:T(8,128)(2,1)S(1)}, bf16[3584,128]{1,0:T(8,128)(2,1)S(1)}, u32[]{:S(2)}, u32[]{:S(2)}) collective-permute-start(bf16[3584,128]{1,0:T(8,128)(2,1)S(1)} %collective-permute-done.4), channel_id=1, source_target_pairs={{0,1},{1,2},{2,3},{3,4},{4,5},{5,6},{6,7},{7,8},{8,9},{9,10},{10,1... | collective-permute-start | bytes 2752520 | tf_op jit(solution)/shard_map/ppermute | solution.py:18
  80.6 0.9 copy-start.8
  81.5 14.0 %collective-permute-start.12 = (bf16[3584,128]{1,0:T(8,128)(2,1)S(1)}, bf16[3584,128]{1,0:T(8,128)(2,1)}, u32[]{:S(2)}, u32[]{:S(2)}) collective-permute-start(bf16[3584,128]{1,0:T(8,128)(2,1)S(1)} %collective-permute-done.11), channel_id=1, source_target_pairs={{0,15},{1,0},{2,1},{3,2},{4,3},{5,4},{6,5},{7,6},{8,7},{9,8},{10,9... | collective-permute-start | bytes 2752520 | tf_op jit(solution)/shard_map/ppermute | solution.py:20
  93.6 14.1 %copy-start.14 = (bf16[3584,128]{1,0:T(8,128)(2,1)}, bf16[3584,128]{1,0:T(8,128)(2,1)S(1)}, u32[]{:S(2)}) copy-start(bf16[3584,128]{1,0:T(8,128)(2,1)S(1)} %collective-permute-done.5) | copy-start | bytes 2752516
  93.6 14.1 %collective-permute-start.6 = (bf16[3584,128]{1,0:T(8,128)(2,1)S(1)}, bf16[3584,128]{1,0:T(8,128)(2,1)}, u32[]{:S(2)}, u32[]{:S(2)}) collective-permute-start(bf16[3584,128]{1,0:T(8,128)(2,1)S(1)} %collective-permute-done.5), channel_id=1, source_target_pairs={{0,1},{1,2},{2,3},{3,4},{4,5},{5,6},{6,7},{7,8},{8,9},{9,10},{10,1... | collective-permute-start | bytes 2752520 | tf_op jit(solution)/shard_map/ppermute | solution.py:18
  95.6 14.5 %collective-permute-start.13 = (bf16[3584,128]{1,0:T(8,128)(2,1)}, bf16[3584,128]{1,0:T(8,128)(2,1)}, u32[]{:S(2)}, u32[]{:S(2)}) collective-permute-start(bf16[3584,128]{1,0:T(8,128)(2,1)} %collective-permute-done.12), channel_id=1, source_target_pairs={{0,15},{1,0},{2,1},{3,2},{4,3},{5,4},{6,5},{7,6},{8,7},{9,8},{10,9... | collective-permute-start | bytes 2752520 | tf_op jit(solution)/shard_map/ppermute | solution.py:20
  107.8 14.3 %collective-permute-start.7 = (bf16[3584,128]{1,0:T(8,128)(2,1)}, bf16[3584,128]{1,0:T(8,128)(2,1)}, u32[]{:S(2)}, u32[]{:S(2)}) collective-permute-start(bf16[3584,128]{1,0:T(8,128)(2,1)} %collective-permute-done.6), channel_id=1, source_target_pairs={{0,1},{1,2},{2,3},{3,4},{4,5},{5,6},{6,7},{7,8},{8,9},{9,10},{10,1... | collective-permute-start | bytes 2752520 | tf_op jit(solution)/shard_map/ppermute | solution.py:18
  107.8 51.9 %copy-start.15 = (bf16[3584,128]{1,0:T(8,128)(2,1)S(1)}, bf16[3584,128]{1,0:T(8,128)(2,1)}, u32[]{:S(2)}) copy-start(bf16[3584,128]{1,0:T(8,128)(2,1)} %copy-done.14) | copy-start | bytes 2752516
  107.8 53.1 %copy-start.13 = (bf16[3584,128]{1,0:T(8,128)(2,1)S(1)}, bf16[3584,128]{1,0:T(8,128)(2,1)}, u32[]{:S(2)}) copy-start(bf16[3584,128]{1,0:T(8,128)(2,1)} %copy-done.12) | copy-start | bytes 2752516
  107.8 54.1 %copy-start.11 = (bf16[3584,128]{1,0:T(8,128)(2,1)S(1)}, bf16[3584,128]{1,0:T(8,128)(2,1)}, u32[]{:S(2)}) copy-start(bf16[3584,128]{1,0:T(8,128)(2,1)} %copy-done.10) | copy-start | bytes 2752516
  107.8 55.1 %copy-start.5 = (bf16[3584,128]{1,0:T(8,128)(2,1)S(1)}, bf16[3584,128]{1,0:T(8,128)(2,1)}, u32[]{:S(2)}) copy-start(bf16[3584,128]{1,0:T(8,128)(2,1)} %copy-done.4) | copy-start | bytes 2752516
  107.8 62.8 %copy-start.3 = (bf16[3584,128]{1,0:T(8,128)(2,1)S(1)}, bf16[3584,128]{1,0:T(8,128)(2,1)}, u32[]{:S(2)}) copy-start(bf16[3584,128]{1,0:T(8,128)(2,1)} %copy-done.2) | copy-start | bytes 2752516
  107.8 63.9 %copy-start.7 = (bf16[3584,128]{1,0:T(8,128)(2,1)S(1)}, bf16[3584,128]{1,0:T(8,128)(2,1)}, u32[]{:S(2)}) copy-start(bf16[3584,128]{1,0:T(8,128)(2,1)} %copy-done.6) | copy-start | bytes 2752516
  107.8 65.0 %copy-start.9 = (bf16[3584,128]{1,0:T(8,128)(2,1)S(1)}, bf16[3584,128]{1,0:T(8,128)(2,1)}, u32[]{:S(2)}) copy-start(bf16[3584,128]{1,0:T(8,128)(2,1)} %copy-done.8) | copy-start | bytes 2752516
  109.9 69.6 %copy-start.17 = (bf16[2048,128]{1,0:T(8,128)(2,1)S(1)}, bf16[2048,128]{1,0:T(8,128)(2,1)}, u32[]{:S(2)}) copy-start(bf16[2048,128]{1,0:T(8,128)(2,1)} %param.9) | copy-start | bytes 1572868
  110.0 44.2 %collective-permute-start.14 = (bf16[3584,128]{1,0:T(8,128)(2,1)}, bf16[3584,128]{1,0:T(8,128)(2,1)S(1)}, u32[]{:S(2)}, u32[]{:S(2)}) collective-permute-start(bf16[3584,128]{1,0:T(8,128)(2,1)} %collective-permute-done.13), channel_id=1, source_target_pairs={{0,15},{1,0},{2,1},{3,2},{4,3},{5,4},{6,5},{7,6},{8,7},{9,8},{10,9... | collective-permute-start | bytes 2752520 | tf_op jit(solution)/shard_map/ppermute | solution.py:20
  187.2 77.1 %copy-start.16 = (pred[896,896]{1,0:T(8,128)(4,1)S(1)}, pred[896,896]{1,0:T(8,128)(4,1)}, u32[]{:S(2)}) copy-start(pred[896,896]{1,0:T(8,128)(4,1)} %iota_compare_fusion) | copy-start | bytes 2408452
  200.0 191.0 %reduce-scatter.4.cloned.1.call-start = ((), (), s32[]{:S(2)}) async-start(), calls=%async_computation.2 | async-start | bytes 15597568
Sparse Core Ops, SparseCore 0:
  200.1 47.8 all-gather.5
  302.1 88.8 reduce-scatter.3
